TPU v7x, 128 devices: a whole 4x4x4 slice. The times are simulated.
128 devices in a mesh: space: 32 (over y, x, core), tx: 4 (over z).
Axes of the slice: x: 4, y: 4, z: 4, core: 2. Of those that a mesh axis runs over, the one named last changes fastest.
Arguments:
- conductivity: float32 [64, 128, 256], P('space'), may hold values from 0.25 to 2
- chargeability: float32 [64, 128, 256], P('space'), may hold values from 0.05 to 0.6
- relaxation: float32 [64, 128, 256], P('space'), may hold values from 0.5 to 8
- start_potential: float32 [8, 64, 128, 256], P('tx', 'space'), may hold values from 0 to 2
- start_memory: float32 [4, 8, 64, 128, 256], P(None, 'tx', 'space'), may hold values from -6 to 6
- source_cells: int32 [2, 8], P(None, 'tx'), may hold values from 0 to 2097151
- dipole_cells: int32 [2, 4096], replicated, may hold values from 0 to 2097151
- live_counts: int32 [32], replicated, may hold values from 32 to 128, as said below
- observed: float32 [3, 8, 4096], P(None, 'tx', 'space'), may hold values from -4 to 4
Outputs:
- voltages: float32 [3, 8, 4096], P(None, 'tx', 'space')
- misfit: float32 [], replicated
- grad_chargeability: float32 [64, 128, 256], P('space', 'tx')
- grad_relaxation: float32 [64, 128, 256], P('space', 'tx')
Inputs may be any that keep to these rules, and one draw needn't show every extreme that they name: `source_cells`: flat cell indices of the grid. `dipole_cells`: flat cell indices of the grid. `live_counts`: some slab has all 128 slots live.
All inputs are finite; a program needn't handle non-finite values.
Results may differ from a plain program's by a relative error of at most 0.00002.
Values sent between devices are 32-bit elements; how exact they have to be, the bound alone decides.
A program may use at most 192 MiB of HBM per device.

v0:
```python
import jax
import jax.numpy as jnp
from jax import lax
from jax.sharding import PartitionSpec as P

NSTEPS = 3
JACOBI = 8
mode_weights = (0.4, 0.3, 0.2, 0.1)
mode_ratios = (0.25, 1.0, 4.0, 16.0)
strength = 4.0


def extended(array, sides, width):
    for axis, dim in sides:
        peers, length = (lax.axis_size(axis), array.shape[dim])
        up = [(i, (i + 1) % peers) for i in range(peers - 1)]
        down = [(j, i) for i, j in up]
        last = lax.slice_in_dim(array, length - width, length, axis=dim)
        initial = lax.slice_in_dim(array, 0, width, axis=dim)
        before = lax.ppermute(last, axis, up)
        after = lax.ppermute(initial, axis, down)
        array = jnp.concatenate([before, array, after], axis=dim)
    return array


def neighbours(padded):
    core = padded[:, 1:-1]
    total = padded[:, 2:] + padded[:, :-2]
    side_y = jnp.pad(core, ((0, 0), (0, 0), (1, 1), (0, 0)))
    total = total + side_y[:, :, 2:] + side_y[:, :, :-2]
    side_z = jnp.pad(core, ((0, 0), (0, 0), (0, 0), (1, 1)))
    return total + side_z[..., 2:] + side_z[..., :-2]


def rim_one(field):
    return extended(field, (("space", 1),), 1)


def total_misfit(partial_value):
    return jnp.sqrt(1.0 + lax.psum(partial_value, ("space", "tx")))


def on_device(
    conductivity,
    chargeability,
    relaxation,
    start_potential,
    start_memory,
    source_cells,
    dipole_cells,
    live_counts,
    observed,
):
    slots = start_potential.shape[0]
    cells = conductivity.size
    tile = lax.axis_index("space")
    first = tile * cells
    inverse = 1.0 / (6.0 + conductivity)

    def local_index(global_cells):
        shifted = global_cells - first
        inside = ((shifted >= 0) & (shifted < cells)).astype(jnp.float32)
        return (jnp.clip(shifted, 0, cells - 1), inside)

    slot_ids = jnp.arange(slots, dtype=jnp.int32)
    place_a, inside_a = local_index(source_cells[0])
    place_b, inside_b = local_index(source_cells[1])
    source = jnp.zeros((slots, cells), jnp.float32).at[slot_ids, place_a].add(strength * inside_a)
    source = source.at[slot_ids, place_b].add(-strength * inside_b).reshape(start_potential.shape)
    probe_one, inside_one = local_index(dipole_cells[0])
    probe_two, inside_two = local_index(dipole_cells[1])
    decays = [jnp.exp(-1.0 / (relaxation * ratio)) for ratio in mode_ratios]
    couple = [chargeability * mode_weights[level] * (1.0 - decays[level]) for level in range(4)]
    slopes = [decays[level] / (mode_ratios[level] * relaxation * relaxation) for level in range(4)]
    memory = [start_memory[level] for level in range(4)]
    potential = start_potential
    kept_potential = []
    kept_memory = []
    partials = []
    for step in range(NSTEPS):
        stored = memory[0] + memory[1] + memory[2] + memory[3]
        if step == 0:
            rhs = source + conductivity * stored
        else:
            rhs = conductivity * stored
        forward_field = potential
        for forward_sweep in range(JACOBI):
            forward_field = (rhs + neighbours(rim_one(forward_field))) * inverse
        potential = forward_field
        kept_potential.append(potential)
        kept_memory.append(memory)
        memory = [decays[level] * memory[level] + couple[level] * potential for level in range(4)]
        flat = potential.reshape(slots, cells)
        partials.append(
            jnp.take(flat, probe_one, axis=1) * inside_one
            - jnp.take(flat, probe_two, axis=1) * inside_two
        )
    volts = lax.psum_scatter(jnp.stack(partials), "space", scatter_dimension=2, tiled=True)
    receivers = observed.shape[2]
    live = (jnp.arange(receivers) < live_counts[tile]).astype(jnp.float32)
    volts = volts * live
    resid = live * (volts - observed)
    partial_value = jnp.sum(resid * resid)
    misfit = total_misfit(partial_value)
    pulled = resid / misfit
    spread = lax.all_gather(pulled, "space", axis=2, tiled=True)
    back = jnp.zeros_like(start_potential)
    duals = [jnp.zeros_like(start_potential) for level in range(4)]
    grad_c = jnp.zeros_like(start_potential)
    grad_t = jnp.zeros_like(start_potential)
    for step in reversed(range(NSTEPS)):
        current = kept_potential[step]
        before = kept_memory[step]
        inject = jnp.zeros((slots, cells), jnp.float32)
        inject = inject.at[:, probe_one].add(spread[step] * inside_one)
        inject = (
            inject.at[:, probe_two].add(-spread[step] * inside_two).reshape(start_potential.shape)
        )
        incoming = back + inject
        for level in range(4):
            incoming = incoming + couple[level] * duals[level]
            grad_c = grad_c + duals[level] * mode_weights[level] * (1.0 - decays[level]) * current
            grad_t = grad_t + duals[level] * slopes[level] * (
                before[level] - chargeability * mode_weights[level] * current
            )
        duals = [decays[level] * duals[level] for level in range(4)]
        field = incoming
        summed = jnp.zeros_like(incoming)
        for sweep in range(JACOBI):
            scaled = field * inverse
            summed = summed + scaled
            field = neighbours(rim_one(scaled))
        summed, back = (summed, field)
        duals = [duals[level] + conductivity * summed for level in range(4)]
    grad_charge, grad_relax = (
        lax.psum_scatter(jnp.sum(grad_c, axis=0), "tx", scatter_dimension=1, tiled=True),
        lax.psum_scatter(jnp.sum(grad_t, axis=0), "tx", scatter_dimension=1, tiled=True),
    )
    return (volts, misfit, grad_charge, grad_relax)


def solution(mesh):
    placed = (
        P("space", None, None),
        P("space", None, None),
        P("space", None, None),
        P("tx", "space", None, None),
        P(None, "tx", "space", None, None),
        P(None, "tx"),
        P(),
        P(),
        P(None, "tx", "space"),
    )
    return jax.shard_map(
        on_device,
        mesh=mesh,
        in_specs=placed,
        out_specs=(P(None, "tx", "space"), P(), P("space", "tx", None), P("space", "tx", None)),
        check_vma=False,
    )
```

profile of v0, /device:TPU:0, one launch (start us, length us, event | category | flops | bytes accessed | tf_op | source)
XLA Modules:
  0.0 1156.9 jit_solution(7150294656307960920)
XLA Ops:
  27.8 7.2 collective-permute-start.5
  37.8 7.2 collective-permute-start.7
  47.8 7.2 collective-permute-start.9
  57.9 7.2 collective-permute-start.11
  67.9 7.2 collective-permute-start.13
  78.1 7.2 collective-permute-start.15
  88.1 7.2 collective-permute-start.17
  108.6 7.2 collective-permute-start.21
  118.6 7.2 collective-permute-start.23
  128.6 7.2 collective-permute-start.25
  138.7 7.2 collective-permute-start.27
  148.7 9.1 collective-permute-start.29
  160.7 7.4 collective-permute-start.31
  171.0 9.5 collective-permute-start.33
  183.8 9.3 collective-permute-start.35
  195.9 9.3 collective-permute-start.37
  208.0 9.3 collective-permute-start.39
  220.2 9.3 collective-permute-start.41
  232.4 9.3 collective-permute-start.43
  244.5 9.3 collective-permute-start.45
  258.2 10.0 collective-permute-start.47
  268.2 16.6 %copy.44 = f32[2,2,128,256]{0,3,2,1:T(8,128)} copy(f32[2,2,128,256]{3,2,1,0:T(8,128)S(1)} %fusion.73) | data formatting | bytes 1048576 | tf_op jit(solution)/shard_map/mul | solution.py:88
  284.8 24.7 %gather_fusion.1 = f32[4096,2]{1,0:T(8,128)} fusion(f32[2,65536]{0,1:T(8,128)} %bitcast.195, s32[4096]{0:T(1024)S(1)} %fusion.321), kind=kCustom, calls=%fused_computation.1.clone | custom fusion | bytes 81920 | tf_op jit(solution)/shard_map/jit(_take)/gather | solution.py:96
  309.5 24.7 %gather_fusion = f32[4096,2]{1,0:T(8,128)} fusion(f32[2,65536]{0,1:T(8,128)} %bitcast.196, s32[4096]{0:T(1024)S(1)} %fusion.320), kind=kCustom, calls=%fused_computation.clone | custom fusion | bytes 81920 | tf_op jit(solution)/shard_map/jit(_take)/gather | solution.py:95
  334.2 17.4 %copy.45 = f32[2,2,128,256]{0,3,2,1:T(8,128)} copy(f32[2,2,128,256]{3,2,1,0:T(8,128)} %copy-done.1) | data formatting | bytes 1048576 | tf_op jit(solution)/shard_map/mul | solution.py:88
  351.6 24.7 %gather_fusion.3 = f32[4096,2]{1,0:T(8,128)} fusion(f32[2,65536]{0,1:T(8,128)} %bitcast.197, s32[4096]{0:T(1024)S(1)} %fusion.321), kind=kCustom, calls=%fused_computation.3.clone | custom fusion | bytes 81920 | tf_op jit(solution)/shard_map/jit(_take)/gather | solution.py:96
  376.4 24.7 %gather_fusion.2 = f32[4096,2]{1,0:T(8,128)} fusion(f32[2,65536]{0,1:T(8,128)} %bitcast.198, s32[4096]{0:T(1024)S(1)} %fusion.320), kind=kCustom, calls=%fused_computation.2.clone | custom fusion | bytes 81920 | tf_op jit(solution)/shard_map/jit(_take)/gather | solution.py:95
  404.7 17.4 %copy.46 = f32[2,2,128,256]{0,3,2,1:T(8,128)} copy(f32[2,2,128,256]{3,2,1,0:T(8,128)} %fusion.169) | data formatting | bytes 1048576 | tf_op jit(solution)/shard_map/mul | solution.py:88
  422.2 24.7 %gather_fusion.5 = f32[4096,2]{1,0:T(8,128)} fusion(f32[2,65536]{0,1:T(8,128)} %bitcast.193, s32[4096]{0:T(1024)S(1)} %fusion.321), kind=kCustom, calls=%fused_computation.5.clone | custom fusion | bytes 81920 | tf_op jit(solution)/shard_map/jit(_take)/gather | solution.py:96
  446.9 24.7 %gather_fusion.4 = f32[4096,2]{1,0:T(8,128)} fusion(f32[2,65536]{0,1:T(8,128)} %bitcast.194, s32[4096]{0:T(1024)S(1)} %fusion.320), kind=kCustom, calls=%fused_computation.4.clone | custom fusion | bytes 81920 | tf_op jit(solution)/shard_map/jit(_take)/gather | solution.py:95
  482.5 119.5 %reduce-scatter.4.cloned.1.call-done = f32[3,2,128]{1,2,0:T(8,128)} async-done(((f32[3,2,4096]{1,2,0:T(8,128)}), f32[3,2,128]{1,2,0:T(8,128)}) %reduce-scatter.4.cloned.1.call-update) | async-done | bytes 3088 | tf_op jit(solution)/shard_map/reduce_scatter | solution.py:98
  603.7 64.8 %psum.7 = f32[]{:T(128)} all-reduce(f32[]{:T(128)} %multiply_reduce_fusion), channel_id=1, replica_groups=mesh['space'=32,'tx'=4] {'space','tx'}, use_global_device_ids=true, to_apply=%region_4.6 | all-reduce | flops 1 | bytes 8 | tf_op jit(solution)/shard_map/psum | solution.py:40
  671.0 31.1 %all_gather.3 = f32[3,2,4096]{1,2,0:T(8,128)} all-gather(f32[3,2,128]{1,2,0:T(8,128)S(1)} %get-tuple-element.175), channel_id=1, replica_groups=mesh['space'=32,'tx'=4] {'space'}, dimensions={2}, use_global_device_ids=true | all-gather | bytes 101376 | tf_op jit(solution)/shard_map/all_gather | solution.py:106
  702.1 43.5 %scatter_custom_fusion.2 = f32[2,65536]{0,1:T(8,128)} fusion(s32[4096]{0:T(1024)S(1)} %bitcast.213, f32[]{:T(128)} %constant.26.clone.1, f32[3,2,4096]{1,2,0:T(8,128)} %all_gather.3, f32[4096]{0:T(1024)S(1)} %bitcast.205), kind=kCustom, calls=%fused_computation.14 | custom fusion | flops 16384 | bytes 2638336 | tf_op jit(solution)/shard_map/scatter-add | solution.py:115
  745.6 51.9 %scatter_custom_fusion.3 = f32[2,65536]{0,1:T(8,128)} fusion(f32[2,65536]{0,1:T(8,128)} %scatter_custom_fusion.2, s32[4096]{0:T(1024)S(1)} %bitcast.211, f32[3,2,4096]{1,2,0:T(8,128)} %all_gather.3, f32[4096]{0:T(1024)S(1)} %bitcast.202), kind=kCustom, calls=%fused_computation.22 | custom fusion | flops 24576 | bytes 2637824 | tf_op jit(solution)/shard_map/scatter-add | solution.py:117
  797.6 19.4 %copy.49 = f32[2,2,128,256]{3,2,1,0:T(8,128)S(1)} copy(f32[2,2,128,256]{0,3,2,1:T(8,128)} %bitcast.192) | data formatting | bytes 1048576 | tf_op jit(solution)/shard_map/reshape | solution.py:117
  833.3 7.2 collective-permute-start.53
  873.4 7.2 collective-permute-start.61
  884.4 7.9 collective-permute-start.63
  892.3 43.7 %scatter_custom_fusion.4 = f32[2,65536]{0,1:T(8,128)} fusion(s32[4096]{0:T(1024)S(1)} %bitcast.214, f32[]{:T(128)} %constant.26.clone.1, f32[3,2,4096]{1,2,0:T(8,128)} %all_gather.3, f32[4096]{0:T(1024)S(1)} %bitcast.206), kind=kCustom, calls=%fused_computation.12 | custom fusion | flops 16384 | bytes 2638336 | tf_op jit(solution)/shard_map/scatter-add | solution.py:115
  935.9 51.9 %scatter_custom_fusion.5 = f32[2,65536]{0,1:T(8,128)} fusion(f32[2,65536]{0,1:T(8,128)} %scatter_custom_fusion.4, s32[4096]{0:T(1024)S(1)} %bitcast.212, f32[3,2,4096]{1,2,0:T(8,128)} %all_gather.3, f32[4096]{0:T(1024)S(1)} %bitcast.203), kind=kCustom, calls=%fused_computation.19 | custom fusion | flops 24576 | bytes 2637824 | tf_op jit(solution)/shard_map/scatter-add | solution.py:117
  987.9 20.2 %copy.51 = f32[2,2,128,256]{3,2,1,0:T(8,128)} copy(f32[2,2,128,256]{0,3,2,1:T(8,128)} %bitcast.191) | data formatting | bytes 1048576 | tf_op jit(solution)/shard_map/reshape | solution.py:117
  1008.1 8.1 fusion.214
  1052.5 7.2 collective-permute-start.73
  1063.0 7.2 collective-permute-start.75
  1073.0 7.2 collective-permute-start.77
  1091.9 33.7 %reduce-scatter.8.cloned.1.call-done = f32[2,32,256]{2,1,0:T(8,128)} async-done(((f32[2,128,256]{2,1,0:T(8,128)}), f32[2,32,256]{2,1,0:T(8,128)}) %reduce-scatter.8.cloned.1.call-update) | async-done | bytes 65552 | tf_op jit(solution)/shard_map/reduce_scatter | solution.py:137
  1125.6 23.5 %reduce-scatter.6.cloned.1.call-done = f32[2,32,256]{2,1,0:T(8,128)} async-done(((f32[2,128,256]{2,1,0:T(8,128)}), f32[2,32,256]{2,1,0:T(8,128)}) %reduce-scatter.6.cloned.1.call-update) | async-done | bytes 65552 | tf_op jit(solution)/shard_map/reduce_scatter | solution.py:136
  (355 shorter events, 213.1 us)
Async XLA Ops:
  7.2 594.9 %reduce-scatter.4.cloned.1.call-start = ((), (), s32[]{:S(2)}) async-start(), calls=%async_computation.3 | async-start | bytes 6488064 | tf_op jit(solution)/shard_map/reduce_scatter | solution.py:98
  26.5 8.5 collective-permute-start.4
  36.5 8.5 collective-permute-start.6
  46.5 8.5 collective-permute-start.8
  56.6 8.5 collective-permute-start.10
  66.6 8.5 collective-permute-start.12
  76.7 8.6 collective-permute-start.14
  86.8 11.5 collective-permute-start.16
  88.1 10.2 collective-permute-start.17
  107.3 8.5 collective-permute-start.20
  117.3 8.5 collective-permute-start.22
  127.3 8.5 collective-permute-start.24
  137.4 8.5 collective-permute-start.26
  147.4 10.4 collective-permute-start.28
  148.7 10.2 collective-permute-start.29
  159.3 8.9 collective-permute-start.30
  160.7 8.6 collective-permute-start.31
  169.7 10.8 collective-permute-start.32
  171.0 10.4 collective-permute-start.33
  182.5 10.6 collective-permute-start.34
  183.8 10.4 collective-permute-start.35
  194.6 10.6 collective-permute-start.36
  195.9 10.4 collective-permute-start.37
  206.7 10.6 collective-permute-start.38
  208.0 10.4 collective-permute-start.39
  218.9 10.6 collective-permute-start.40
  220.2 10.4 collective-permute-start.41
  231.1 10.7 collective-permute-start.42
  232.4 10.4 collective-permute-start.43
  243.2 10.7 collective-permute-start.44
  244.5 10.4 collective-permute-start.45
  256.9 144.2 %collective-permute-start.46 = (f32[2,1,128,256]{3,2,1,0:T(8,128)}, f32[2,1,128,256]{3,2,1,0:T(8,128)}, u32[]{:S(2)}, u32[]{:S(2)}) collective-permute-start(f32[2,1,128,256]{3,2,1,0:T(8,128)} %get-tuple-element.81), channel_id=1, source_target_pairs={{4,0},{8,4},{12,8},{16,12},{20,16},{24,20},{28,24},{32,28},{36,32}... | collective-permute-start | bytes 786440 | tf_op jit(solution)/shard_map/ppermute | solution.py:21
  258.2 142.9 %collective-permute-start.47 = (f32[2,1,128,256]{3,2,1,0:T(8,128)}, f32[2,1,128,256]{3,2,1,0:T(8,128)}, u32[]{:S(2)}, u32[]{:S(2)}) collective-permute-start(f32[2,1,128,256]{3,2,1,0:T(8,128)} %get-tuple-element.82), channel_id=1, source_target_pairs={{0,4},{4,8},{8,12},{12,16},{16,20},{20,24},{24,28},{28,32},{32,36}... | collective-permute-start | bytes 786440 | tf_op jit(solution)/shard_map/ppermute | solution.py:20
  480.5 645.1 %reduce-scatter.8.cloned.1.call-start = ((), (), s32[]{:S(2)}) async-start(), calls=%async_computation.5 | async-start | bytes 327680 | tf_op jit(solution)/shard_map/reduce_scatter | solution.py:137
  832.0 8.5 collective-permute-start.52
  842.0 8.5 collective-permute-start.54
  852.1 8.5 collective-permute-start.56
  862.1 8.5 collective-permute-start.58
  872.1 8.5 collective-permute-start.60
  883.1 125.0 %collective-permute-start.62 = (f32[2,1,128,256]{3,2,1,0:T(8,128)}, f32[2,1,128,256]{3,2,1,0:T(8,128)}, u32[]{:S(2)}, u32[]{:S(2)}) collective-permute-start(f32[2,1,128,256]{3,2,1,0:T(8,128)} %get-tuple-element.65), channel_id=1, source_target_pairs={{4,0},{8,4},{12,8},{16,12},{20,16},{24,20},{28,24},{32,28},{36,32}... | collective-permute-start | bytes 786440 | tf_op jit(solution)/shard_map/ppermute | solution.py:21
  884.4 123.7 %collective-permute-start.63 = (f32[2,1,128,256]{3,2,1,0:T(8,128)}, f32[2,1,128,256]{3,2,1,0:T(8,128)}, u32[]{:S(2)}, u32[]{:S(2)}) collective-permute-start(f32[2,1,128,256]{3,2,1,0:T(8,128)} %get-tuple-element.66), channel_id=1, source_target_pairs={{0,4},{4,8},{8,12},{12,16},{16,20},{20,24},{24,28},{28,32},{32,36}... | collective-permute-start | bytes 786440 | tf_op jit(solution)/shard_map/ppermute | solution.py:20
  1031.0 8.5 collective-permute-start.68
  1041.0 8.5 collective-permute-start.70
  1051.1 8.6 collective-permute-start.72
  1061.4 8.8 collective-permute-start.74
  1071.7 8.5 collective-permute-start.76
  1073.0 8.3 collective-permute-start.77
  1087.2 61.8 %reduce-scatter.6.cloned.1.call-start = ((), (), s32[]{:S(2)}) async-start(), calls=%async_computation.4 | async-start | bytes 327680 | tf_op jit(solution)/shard_map/reduce_scatter | solution.py:136
  (93 other events, 1863.3 us)
Sparse Core Ops, SparseCore 0:
  480.6 121.4 reduce-scatter.3
  1087.4 38.1 reduce-scatter.7
  1128.5 20.4 reduce-scatter.5
where the time goes:
time: 1170 us; the launch traced here: 1160 us
  starting transfers between devices  332 us (28%)
  other arithmetic  249 us (21%)
  local copies, waits for them, and re-layouts  248 us (21%)
  waiting for transfers between devices  215 us (18%)
  blocking collectives  96 us (8%)
  between operations  18 us (2%)
    ppermute x39, starting transfers between devices, extended(): before = lax.ppermute(last, axis, up)  280 us
    reduce_scatter x1, waiting for transfers between devices, on_device(): lax.psum_scatter(jnp.stack(partials), 'space', scatter_dimension=2, tiled...  120 us
    scatter-add x2, other arithmetic, on_device(): inject.at[:, probe_two].add(-spread[step] * inside_two)  104 us
    scatter-add x2, other arithmetic, on_device(): inject = inject.at[:, probe_one].add(spread[step] * inside_one)  87.2 us
    gather x3, local copies, waits for them, and re-layouts, on_device(): jnp.take(flat, probe_one, axis=1) * inside_one  74.2 us
    gather x3, local copies, waits for them, and re-layouts, on_device(): jnp.take(flat, probe_two, axis=1) * inside_two  74.1 us
    psum x1, blocking collectives, total_misfit(): return jnp.sqrt(1.0 + lax.psum(partial_value, ('space', 'tx')))  64.8 us
    mul x3, local copies, waits for them, and re-layouts, on_device(): forward_field = (rhs + neighbours(rim_one(forward_field))) * inverse  51.4 us
  transfers between devices with their start and end apart: 81, of which 38 were waited for; matrix products, arithmetic and copies ran while one was open for 23% of the time, Pallas kernels for 0%

commit v1 on v0

--- a/solution.py
+++ b/solution.py
@@ -37,7 +37,7 @@
 
 
 def total_misfit(partial_value):
-    return jnp.sqrt(1.0 + lax.psum(partial_value, ("space", "tx")))
+    return jnp.sqrt(1.0 + lax.psum(lax.psum(partial_value, "space"), "tx"))
 
 
 def on_device(

time: 1170 us -> 1180 us (level)
    psum x1 -> x2, blocking collectives: 64.8 us -> 75 us  [total_misfit(): return jnp.sqrt(1.0 + lax.psum(lax.psum(partial_value, 'space'), 'tx'))]
  transfers between devices with their start and end apart: 81 -> 81, of which waited for: 38 -> 38; matrix products, arithmetic and copies ran while one was open for 23% -> 22% of each run, Pallas kernels for 0% -> 0%
where the time goes in v1:
time: 1180 us; the launch traced here: 1170 us
  starting transfers between devices  332 us (28%)
  other arithmetic  249 us (21%)
  local copies, waits for them, and re-layouts  247 us (21%)
  waiting for transfers between devices  215 us (18%)
  blocking collectives  106 us (9%)
  between operations  18 us (2%)
    ppermute x39, starting transfers between devices, extended(): before = lax.ppermute(last, axis, up)  280 us
    reduce_scatter x1, waiting for transfers between devices, on_device(): lax.psum_scatter(jnp.stack(partials), 'space', scatter_dimension=2, tiled...  119 us
    scatter-add x2, other arithmetic, on_device(): inject.at[:, probe_two].add(-spread[step] * inside_two)  104 us
    scatter-add x2, other arithmetic, on_device(): inject = inject.at[:, probe_one].add(spread[step] * inside_one)  87.2 us
    psum x2, blocking collectives, total_misfit(): return jnp.sqrt(1.0 + lax.psum(lax.psum(partial_value, 'space'), 'tx'))  75 us
    gather x3, local copies, waits for them, and re-layouts, on_device(): jnp.take(flat, probe_two, axis=1) * inside_two  73.9 us
    gather x3, local copies, waits for them, and re-layouts, on_device(): jnp.take(flat, probe_one, axis=1) * inside_one  73.9 us
    mul x3, local copies, waits for them, and re-layouts, on_device(): forward_field = (rhs + neighbours(rim_one(forward_field))) * inverse  51.2 us
  transfers between devices with their start and end apart: 81, of which 38 were waited for; matrix products, arithmetic and copies ran while one was open for 22% of the time, Pallas kernels for 0%

profile of v1, /device:TPU:0, one launch (start us, length us, event | category | flops | bytes accessed | tf_op | source)
XLA Modules:
  0.0 1166.0 jit_solution(10166218158989652179)
XLA Ops:
  27.8 7.2 collective-permute-start.5
  37.8 7.2 collective-permute-start.7
  47.8 7.2 collective-permute-start.9
  57.9 7.2 collective-permute-start.11
  67.9 7.2 collective-permute-start.13
  78.1 7.2 collective-permute-start.15
  88.1 7.2 collective-permute-start.17
  108.6 7.2 collective-permute-start.21
  118.6 7.2 collective-permute-start.23
  128.6 7.2 collective-permute-start.25
  138.7 7.2 collective-permute-start.27
  148.7 9.0 collective-permute-start.29
  160.7 7.5 collective-permute-start.31
  171.1 9.5 collective-permute-start.33
  183.8 9.3 collective-permute-start.35
  195.9 9.3 collective-permute-start.37
  208.1 9.3 collective-permute-start.39
  220.2 9.3 collective-permute-start.41
  232.4 9.3 collective-permute-start.43
  244.5 9.3 collective-permute-start.45
  258.2 10.0 collective-permute-start.47
  268.2 16.5 %copy.44 = f32[2,2,128,256]{0,3,2,1:T(8,128)} copy(f32[2,2,128,256]{3,2,1,0:T(8,128)S(1)} %fusion.73) | data formatting | bytes 1048576 | tf_op jit(solution)/shard_map/mul | solution.py:88
  284.7 24.7 %gather_fusion.1 = f32[4096,2]{1,0:T(8,128)} fusion(f32[2,65536]{0,1:T(8,128)} %bitcast.195, s32[4096]{0:T(1024)S(1)} %fusion.321), kind=kCustom, calls=%fused_computation.1.clone | custom fusion | bytes 81920 | tf_op jit(solution)/shard_map/jit(_take)/gather | solution.py:96
  309.4 24.6 %gather_fusion = f32[4096,2]{1,0:T(8,128)} fusion(f32[2,65536]{0,1:T(8,128)} %bitcast.196, s32[4096]{0:T(1024)S(1)} %fusion.320), kind=kCustom, calls=%fused_computation.clone | custom fusion | bytes 81920 | tf_op jit(solution)/shard_map/jit(_take)/gather | solution.py:95
  334.1 17.3 %copy.45 = f32[2,2,128,256]{0,3,2,1:T(8,128)} copy(f32[2,2,128,256]{3,2,1,0:T(8,128)} %copy-done.1) | data formatting | bytes 1048576 | tf_op jit(solution)/shard_map/mul | solution.py:88
  351.4 24.6 %gather_fusion.3 = f32[4096,2]{1,0:T(8,128)} fusion(f32[2,65536]{0,1:T(8,128)} %bitcast.197, s32[4096]{0:T(1024)S(1)} %fusion.321), kind=kCustom, calls=%fused_computation.3.clone | custom fusion | bytes 81920 | tf_op jit(solution)/shard_map/jit(_take)/gather | solution.py:96
  376.0 24.6 %gather_fusion.2 = f32[4096,2]{1,0:T(8,128)} fusion(f32[2,65536]{0,1:T(8,128)} %bitcast.198, s32[4096]{0:T(1024)S(1)} %fusion.320), kind=kCustom, calls=%fused_computation.2.clone | custom fusion | bytes 81920 | tf_op jit(solution)/shard_map/jit(_take)/gather | solution.py:95
  404.1 17.3 %copy.46 = f32[2,2,128,256]{0,3,2,1:T(8,128)} copy(f32[2,2,128,256]{3,2,1,0:T(8,128)} %fusion.169) | data formatting | bytes 1048576 | tf_op jit(solution)/shard_map/mul | solution.py:88
  421.5 24.6 %gather_fusion.5 = f32[4096,2]{1,0:T(8,128)} fusion(f32[2,65536]{0,1:T(8,128)} %bitcast.193, s32[4096]{0:T(1024)S(1)} %fusion.321), kind=kCustom, calls=%fused_computation.5.clone | custom fusion | bytes 81920 | tf_op jit(solution)/shard_map/jit(_take)/gather | solution.py:96
  446.1 24.6 %gather_fusion.4 = f32[4096,2]{1,0:T(8,128)} fusion(f32[2,65536]{0,1:T(8,128)} %bitcast.194, s32[4096]{0:T(1024)S(1)} %fusion.320), kind=kCustom, calls=%fused_computation.4.clone | custom fusion | bytes 81920 | tf_op jit(solution)/shard_map/jit(_take)/gather | solution.py:95
  481.7 119.5 %reduce-scatter.4.cloned.1.call-done = f32[3,2,128]{1,2,0:T(8,128)} async-done(((f32[3,2,4096]{1,2,0:T(8,128)}), f32[3,2,128]{1,2,0:T(8,128)}) %reduce-scatter.4.cloned.1.call-update) | async-done | bytes 3088 | tf_op jit(solution)/shard_map/reduce_scatter | solution.py:98
  602.8 63.7 %psum.14 = f32[]{:T(128)} all-reduce(f32[]{:T(128)} %multiply_reduce_fusion), channel_id=1, replica_groups=mesh['space'=32,'tx'=4] {'space'}, use_global_device_ids=true, to_apply=%region_4.6 | all-reduce | flops 1 | bytes 8 | tf_op jit(solution)/shard_map/psum | solution.py:40
  666.5 11.3 psum.15
  680.2 31.2 %all_gather.3 = f32[3,2,4096]{1,2,0:T(8,128)} all-gather(f32[3,2,128]{1,2,0:T(8,128)S(1)} %get-tuple-element.175), channel_id=1, replica_groups=mesh['space'=32,'tx'=4] {'space'}, dimensions={2}, use_global_device_ids=true | all-gather | bytes 101376 | tf_op jit(solution)/shard_map/all_gather | solution.py:106
  711.4 43.5 %scatter_custom_fusion.2 = f32[2,65536]{0,1:T(8,128)} fusion(s32[4096]{0:T(1024)S(1)} %bitcast.213, f32[]{:T(128)} %constant.26.clone.1, f32[3,2,4096]{1,2,0:T(8,128)} %all_gather.3, f32[4096]{0:T(1024)S(1)} %bitcast.205), kind=kCustom, calls=%fused_computation.14 | custom fusion | flops 16384 | bytes 2638336 | tf_op jit(solution)/shard_map/scatter-add | solution.py:115
  755.0 51.9 %scatter_custom_fusion.3 = f32[2,65536]{0,1:T(8,128)} fusion(f32[2,65536]{0,1:T(8,128)} %scatter_custom_fusion.2, s32[4096]{0:T(1024)S(1)} %bitcast.211, f32[3,2,4096]{1,2,0:T(8,128)} %all_gather.3, f32[4096]{0:T(1024)S(1)} %bitcast.202), kind=kCustom, calls=%fused_computation.22 | custom fusion | flops 24576 | bytes 2637824 | tf_op jit(solution)/shard_map/scatter-add | solution.py:117
  806.9 19.4 %copy.49 = f32[2,2,128,256]{3,2,1,0:T(8,128)S(1)} copy(f32[2,2,128,256]{0,3,2,1:T(8,128)} %bitcast.192) | data formatting | bytes 1048576 | tf_op jit(solution)/shard_map/reshape | solution.py:117
  842.7 7.2 collective-permute-start.53
  852.7 7.2 collective-permute-start.55
  893.8 7.9 collective-permute-start.63
  901.6 43.7 %scatter_custom_fusion.4 = f32[2,65536]{0,1:T(8,128)} fusion(s32[4096]{0:T(1024)S(1)} %bitcast.214, f32[]{:T(128)} %constant.26.clone.1, f32[3,2,4096]{1,2,0:T(8,128)} %all_gather.3, f32[4096]{0:T(1024)S(1)} %bitcast.206), kind=kCustom, calls=%fused_computation.12 | custom fusion | flops 16384 | bytes 2638336 | tf_op jit(solution)/shard_map/scatter-add | solution.py:115
  945.3 51.9 %scatter_custom_fusion.5 = f32[2,65536]{0,1:T(8,128)} fusion(f32[2,65536]{0,1:T(8,128)} %scatter_custom_fusion.4, s32[4096]{0:T(1024)S(1)} %bitcast.212, f32[3,2,4096]{1,2,0:T(8,128)} %all_gather.3, f32[4096]{0:T(1024)S(1)} %bitcast.203), kind=kCustom, calls=%fused_computation.19 | custom fusion | flops 24576 | bytes 2637824 | tf_op jit(solution)/shard_map/scatter-add | solution.py:117
  997.3 20.2 %copy.51 = f32[2,2,128,256]{3,2,1,0:T(8,128)} copy(f32[2,2,128,256]{0,3,2,1:T(8,128)} %bitcast.191) | data formatting | bytes 1048576 | tf_op jit(solution)/shard_map/reshape | solution.py:117
  1017.5 8.2 fusion.214
  1041.8 7.2 collective-permute-start.69
  1082.5 7.2 collective-permute-start.77
  1101.4 33.3 %reduce-scatter.8.cloned.1.call-done = f32[2,32,256]{2,1,0:T(8,128)} async-done(((f32[2,128,256]{2,1,0:T(8,128)}), f32[2,32,256]{2,1,0:T(8,128)}) %reduce-scatter.8.cloned.1.call-update) | async-done | bytes 65552 | tf_op jit(solution)/shard_map/reduce_scatter | solution.py:137
  1134.7 23.5 %reduce-scatter.6.cloned.1.call-done = f32[2,32,256]{2,1,0:T(8,128)} async-done(((f32[2,128,256]{2,1,0:T(8,128)}), f32[2,32,256]{2,1,0:T(8,128)}) %reduce-scatter.6.cloned.1.call-update) | async-done | bytes 65552 | tf_op jit(solution)/shard_map/reduce_scatter | solution.py:136
  (356 shorter events, 220.1 us)
Async XLA Ops:
  7.2 594.0 %reduce-scatter.4.cloned.1.call-start = ((), (), s32[]{:S(2)}) async-start(), calls=%async_computation.3 | async-start | bytes 6488064 | tf_op jit(solution)/shard_map/reduce_scatter | solution.py:98
  26.5 8.5 collective-permute-start.4
  36.5 8.5 collective-permute-start.6
  46.5 8.5 collective-permute-start.8
  56.6 8.5 collective-permute-start.10
  66.6 8.5 collective-permute-start.12
  76.7 8.6 collective-permute-start.14
  86.8 11.4 collective-permute-start.16
  88.1 10.1 collective-permute-start.17
  107.3 8.5 collective-permute-start.20
  117.3 8.5 collective-permute-start.22
  127.3 8.5 collective-permute-start.24
  137.4 8.5 collective-permute-start.26
  147.4 10.3 collective-permute-start.28
  148.7 10.1 collective-permute-start.29
  159.3 8.9 collective-permute-start.30
  160.7 8.6 collective-permute-start.31
  169.8 10.8 collective-permute-start.32
  171.1 10.4 collective-permute-start.33
  182.5 10.6 collective-permute-start.34
  183.8 10.4 collective-permute-start.35
  194.6 10.6 collective-permute-start.36
  195.9 10.4 collective-permute-start.37
  206.8 10.6 collective-permute-start.38
  208.1 10.4 collective-permute-start.39
  218.9 10.6 collective-permute-start.40
  220.2 10.4 collective-permute-start.41
  231.1 10.7 collective-permute-start.42
  232.4 10.4 collective-permute-start.43
  243.2 10.7 collective-permute-start.44
  244.5 10.4 collective-permute-start.45
  256.9 143.7 %collective-permute-start.46 = (f32[2,1,128,256]{3,2,1,0:T(8,128)}, f32[2,1,128,256]{3,2,1,0:T(8,128)}, u32[]{:S(2)}, u32[]{:S(2)}) collective-permute-start(f32[2,1,128,256]{3,2,1,0:T(8,128)} %get-tuple-element.81), channel_id=1, source_target_pairs={{4,0},{8,4},{12,8},{16,12},{20,16},{24,20},{28,24},{32,28},{36,32}... | collective-permute-start | bytes 786440 | tf_op jit(solution)/shard_map/ppermute | solution.py:21
  258.2 142.5 %collective-permute-start.47 = (f32[2,1,128,256]{3,2,1,0:T(8,128)}, f32[2,1,128,256]{3,2,1,0:T(8,128)}, u32[]{:S(2)}, u32[]{:S(2)}) collective-permute-start(f32[2,1,128,256]{3,2,1,0:T(8,128)} %get-tuple-element.82), channel_id=1, source_target_pairs={{0,4},{4,8},{8,12},{12,16},{16,20},{20,24},{24,28},{28,32},{32,36}... | collective-permute-start | bytes 786440 | tf_op jit(solution)/shard_map/ppermute | solution.py:20
  479.6 655.1 %reduce-scatter.8.cloned.1.call-start = ((), (), s32[]{:S(2)}) async-start(), calls=%async_computation.5 | async-start | bytes 327680 | tf_op jit(solution)/shard_map/reduce_scatter | solution.py:137
  841.4 8.5 collective-permute-start.52
  851.4 8.5 collective-permute-start.54
  861.4 8.5 collective-permute-start.56
  871.5 8.5 collective-permute-start.58
  881.5 8.5 collective-permute-start.60
  892.5 125.0 %collective-permute-start.62 = (f32[2,1,128,256]{3,2,1,0:T(8,128)}, f32[2,1,128,256]{3,2,1,0:T(8,128)}, u32[]{:S(2)}, u32[]{:S(2)}) collective-permute-start(f32[2,1,128,256]{3,2,1,0:T(8,128)} %get-tuple-element.65), channel_id=1, source_target_pairs={{4,0},{8,4},{12,8},{16,12},{20,16},{24,20},{28,24},{32,28},{36,32}... | collective-permute-start | bytes 786440 | tf_op jit(solution)/shard_map/ppermute | solution.py:21
  893.8 123.7 %collective-permute-start.63 = (f32[2,1,128,256]{3,2,1,0:T(8,128)}, f32[2,1,128,256]{3,2,1,0:T(8,128)}, u32[]{:S(2)}, u32[]{:S(2)}) collective-permute-start(f32[2,1,128,256]{3,2,1,0:T(8,128)} %get-tuple-element.66), channel_id=1, source_target_pairs={{0,4},{4,8},{8,12},{12,16},{16,20},{20,24},{24,28},{28,32},{32,36}... | collective-permute-start | bytes 786440 | tf_op jit(solution)/shard_map/ppermute | solution.py:20
  1040.5 8.5 collective-permute-start.68
  1050.6 8.5 collective-permute-start.70
  1060.6 8.6 collective-permute-start.72
  1070.9 8.8 collective-permute-start.74
  1081.2 8.5 collective-permute-start.76
  1082.5 8.3 collective-permute-start.77
  1096.7 61.4 %reduce-scatter.6.cloned.1.call-start = ((), (), s32[]{:S(2)}) async-start(), calls=%async_computation.4 | async-start | bytes 327680 | tf_op jit(solution)/shard_map/reduce_scatter | solution.py:136
  (93 other events, 1863.7 us)
Sparse Core Ops, SparseCore 0:
  479.7 121.3 reduce-scatter.3
  1096.8 37.7 reduce-scatter.7
  1137.6 20.4 reduce-scatter.5
